TPU v7x, 32 devices: a whole 2x2x4 slice. The times are simulated.
32 devices in a mesh: rep: 4 (over z), fsdp: 8 (over y, x, core).
Axes of the slice: x: 2, y: 2, z: 4, core: 2. Of those that a mesh axis runs over, the one named last changes fastest.
Arguments:
- tokens: bfloat16 [4096, 2048], P(('rep', 'fsdp')), may hold values from -6 to 6
- cotangent: bfloat16 [4096, 2048], P(('rep', 'fsdp')), may hold values from -6 to 6
- doc_lengths: int32 [4, 8], replicated, may hold values from 1 to 513, as said below
- norm1_gain: bfloat16 [2048], P('fsdp'), may hold values from 0.5 to 1.5
- w_query: bfloat16 [2048, 2048], P('fsdp'), may hold values from -0.125 to 0.125
- w_key: bfloat16 [2048, 256], P('fsdp'), may hold values from -0.125 to 0.125
- w_value: bfloat16 [2048, 256], P('fsdp'), may hold values from -0.125 to 0.125
- w_out: bfloat16 [2048, 2048], P('fsdp'), may hold values from -0.5 to 0.5
- norm2_gain: bfloat16 [2048], P('fsdp'), may hold values from 0.5 to 1.5
- w_gate: bfloat16 [2048, 5632], P('fsdp'), may hold values from -0.125 to 0.125
- w_up: bfloat16 [2048, 5632], P('fsdp'), may hold values from -0.125 to 0.125
- w_down: bfloat16 [5632, 2048], P('fsdp'), may hold values from -0.078125 to 0.078125
Outputs:
- output: bfloat16 [4096, 2048], P(('rep', 'fsdp'))
- grad_input: bfloat16 [4096, 2048], P(('rep', 'fsdp'))
- grad_norm1: float32 [2048], P('fsdp')
- grad_query: float32 [2048, 2048], P('fsdp')
- grad_key: float32 [2048, 256], P('fsdp')
- grad_value: float32 [2048, 256], P('fsdp')
- grad_out_proj: float32 [2048, 2048], P('fsdp')
- grad_norm2: float32 [2048], P('fsdp')
- grad_gate: float32 [2048, 5632], P('fsdp')
- grad_up: float32 [2048, 5632], P('fsdp')
- grad_down: float32 [5632, 2048], P('fsdp')
Inputs may be any that keep to these rules, and one draw needn't show every extreme that they name: `doc_lengths`: row s lists in order the lengths of the documents packed into sequence s, and as its last entry the length of the tail padding, at most 128; each row sums to 1024, and in each row exactly one document has 513 tokens.
All inputs are finite; a program needn't handle non-finite values.
Results may differ from a plain program's by a relative error of at most 0.022.
Values may be sent and summed in bfloat16 or wider, within the bound.
No kernel may reach another device: no remote copies, remote signals or barrier semaphores. Data moves between devices by JAX's collectives and lax.ppermute only.
A program may use at most 384 MiB of HBM per device.

v0:
```python
import math
import jax
import jax.numpy as jnp
from jax import lax
from jax.sharding import PartitionSpec as P

D = 2048
H = 32
KVH = 4
HD = 64
FF = 5632
DOCS = 8
NORM_EPS = 1e-05
ROPE_BASE = 10000.0
MASK_FILL = -1e30


def angle_tables(positions, head_dim):
    fractions = jnp.arange(0, head_dim, 2, dtype=jnp.float32) / head_dim
    inverse = jnp.exp(-math.log(ROPE_BASE) * fractions)
    angles = positions[:, None] * inverse[None, :]
    angles = jnp.concatenate([angles, angles], axis=-1)
    return (jnp.cos(angles)[:, None, :], jnp.sin(angles)[:, None, :])


def rotate(vectors, cos_table, sin_table):
    half_dim = vectors.shape[-1] // 2
    turned = jnp.concatenate([-vectors[..., half_dim:], vectors[..., :half_dim]], axis=-1)
    return vectors * cos_table + turned * sin_table


def rotate_back(gradients, cos_table, sin_table):
    half_dim = gradients.shape[-1] // 2
    moved = gradients * sin_table
    turned = jnp.concatenate([moved[..., half_dim:], -moved[..., :half_dim]], axis=-1)
    return gradients * cos_table + turned


def masks_for(lengths, offset, tok_count, seq_len):
    bounds = jnp.cumsum(lengths, dtype=jnp.int32)
    key_pos = jnp.arange(seq_len, dtype=jnp.int32)
    key_seg = jnp.sum(
        (bounds[None, :] <= key_pos[:, None]).astype(jnp.int32), axis=1, dtype=jnp.int32
    )
    key_valid = key_seg < DOCS - 1
    query_pos = offset + jnp.arange(tok_count, dtype=jnp.int32)
    query_seg = lax.dynamic_slice_in_dim(key_seg, offset, tok_count)
    query_valid = lax.dynamic_slice_in_dim(key_valid, offset, tok_count)
    allowed = (key_pos[None, :] <= query_pos[:, None]) & (query_seg[:, None] == key_seg[None, :])
    allowed = allowed & query_valid[:, None] & key_valid[None, :] | (
        key_pos[None, :] == query_pos[:, None]
    )
    return (allowed, query_valid, query_pos)


def masked_scores(query_grp, key_grp, allowed):
    score_scale = 1.0 / math.sqrt(query_grp.shape[-1])
    scores = (
        jnp.einsum("tgd,sd->tgs", query_grp, key_grp, preferred_element_type=jnp.float32)
        * score_scale
    )
    return jnp.where(allowed[:, None, :], scores, MASK_FILL)


def attend_forward(query_grp, key_grp, value_grp, allowed):
    scores = masked_scores(query_grp, key_grp, allowed)
    highest = jnp.max(scores, axis=-1, keepdims=True)
    weights = jnp.exp(scores - highest)
    totals = jnp.sum(weights, axis=-1, keepdims=True)
    prob_low = (weights / totals).astype(jnp.bfloat16)
    mixed = jnp.einsum("tgs,sd->tgd", prob_low, value_grp, preferred_element_type=jnp.float32)
    logsum = highest[..., 0] + jnp.log(totals[..., 0])
    return (mixed, logsum)


def attend_backward(query_grp, key_grp, value_grp, allowed, logsum, grad_mixed):
    score_scale = 1.0 / math.sqrt(query_grp.shape[-1])
    scores = masked_scores(query_grp, key_grp, allowed)
    probs_f32 = jnp.exp(scores - logsum[..., None])
    grad_probs = jnp.einsum(
        "tgd,sd->tgs", grad_mixed, value_grp, preferred_element_type=jnp.float32
    )
    inner_sum = jnp.sum(probs_f32 * grad_probs, axis=-1, keepdims=True)
    grad_scores = (probs_f32 * (grad_probs - inner_sum)).astype(jnp.bfloat16)
    grad_query = (
        jnp.einsum("tgs,sd->tgd", grad_scores, key_grp, preferred_element_type=jnp.float32)
        * score_scale
    )
    grad_key = (
        jnp.einsum("tgs,tgd->sd", grad_scores, query_grp, preferred_element_type=jnp.float32)
        * score_scale
    )
    grad_value = jnp.einsum(
        "tgs,tgd->sd",
        probs_f32.astype(jnp.bfloat16),
        grad_mixed,
        preferred_element_type=jnp.float32,
    )
    return (grad_query, grad_key, grad_value)


def norm_parts(vectors):
    scale_inv = lax.rsqrt(jnp.mean(vectors * vectors, axis=-1, keepdims=True) + NORM_EPS)
    return (scale_inv, vectors * scale_inv)


def norm_back(grad_hidden, normed, scale_inv, gain):
    grad_normed = grad_hidden * gain
    return scale_inv * (
        grad_normed - normed * jnp.mean(grad_normed * normed, axis=-1, keepdims=True)
    )


def local(
    tokens,
    cotangent,
    doc_lengths,
    norm1_gain,
    w_query,
    w_key,
    w_value,
    w_out,
    norm2_gain,
    w_gate,
    w_up,
    w_down,
):
    tok_rows = tokens.shape[0]
    group_size = lax.axis_size("fsdp")
    seq_len = tok_rows * group_size
    member = lax.axis_index("fsdp")
    replica = lax.axis_index("rep")
    offset = member * tok_rows
    lengths = lax.dynamic_index_in_dim(doc_lengths, replica, 0, keepdims=False)
    allowed, query_valid, query_pos = masks_for(lengths, offset, tok_rows, seq_len)
    valid_col = query_valid.astype(jnp.float32)[:, None]
    cos_table, sin_table = angle_tables(query_pos.astype(jnp.float32), HD)
    heads_per = H // KVH
    kv_width = KVH * HD
    gain_one, full_query, full_key, full_value, full_out = (
        lax.all_gather(norm1_gain, "fsdp", axis=0, tiled=True),
        lax.all_gather(w_query, "fsdp", axis=0, tiled=True),
        lax.all_gather(w_key, "fsdp", axis=0, tiled=True),
        lax.all_gather(w_value, "fsdp", axis=0, tiled=True),
        lax.all_gather(w_out, "fsdp", axis=0, tiled=True),
    )
    inputs = tokens.astype(jnp.float32)
    scale_one, normed_one = norm_parts(inputs)
    hidden_one = (normed_one * gain_one.astype(jnp.float32)).astype(jnp.bfloat16)
    queries = jnp.dot(hidden_one, full_query, preferred_element_type=jnp.float32).reshape(
        tok_rows, H, HD
    )
    key_proj = jnp.dot(hidden_one, full_key, preferred_element_type=jnp.float32).reshape(
        tok_rows, KVH, HD
    )
    value_low = jnp.dot(hidden_one, full_value, preferred_element_type=jnp.float32).astype(
        jnp.bfloat16
    )
    query_low = rotate(queries, cos_table, sin_table).astype(jnp.bfloat16)
    key_low = (
        rotate(key_proj, cos_table, sin_table).astype(jnp.bfloat16).reshape(tok_rows, kv_width)
    )
    kv_local = jnp.concatenate([key_low, value_low], axis=1)
    kv_seq = lax.all_gather(kv_local, "fsdp", axis=0, tiled=True)
    key_seq = kv_seq[:, :kv_width].reshape(seq_len, KVH, HD).transpose(1, 0, 2)
    value_seq = kv_seq[:, kv_width:].reshape(seq_len, KVH, HD).transpose(1, 0, 2)
    query_grp = query_low.reshape(tok_rows, KVH, heads_per, HD).transpose(1, 0, 2, 3)

    def forward_entry(packed):
        return attend_forward(packed[0], packed[1], packed[2], allowed)

    mixed, logsum = lax.map(forward_entry, (query_grp, key_seq, value_seq))
    attn_low = (mixed.transpose(1, 0, 2, 3).reshape(tok_rows, H * HD) * valid_col).astype(
        jnp.bfloat16
    )
    resid_one = inputs + jnp.dot(attn_low, full_out, preferred_element_type=jnp.float32)
    gain_two, full_gate, full_up, full_down = (
        lax.all_gather(norm2_gain, "fsdp", axis=0, tiled=True),
        lax.all_gather(w_gate, "fsdp", axis=0, tiled=True),
        lax.all_gather(w_up, "fsdp", axis=0, tiled=True),
        lax.all_gather(w_down, "fsdp", axis=0, tiled=True),
    )
    scale_two, normed_two = norm_parts(resid_one)
    hidden_two = (normed_two * gain_two.astype(jnp.float32)).astype(jnp.bfloat16)
    gate_pre = jnp.dot(hidden_two, full_gate, preferred_element_type=jnp.float32)
    up_pre = jnp.dot(hidden_two, full_up, preferred_element_type=jnp.float32)
    sigmoid_gate = jax.nn.sigmoid(gate_pre)
    silu_gate = gate_pre * sigmoid_gate
    inner_low = (silu_gate * up_pre).astype(jnp.bfloat16)
    result = (resid_one + jnp.dot(inner_low, full_down, preferred_element_type=jnp.float32)).astype(
        jnp.bfloat16
    )
    gain_one, full_query, full_key, full_value, full_out = (
        lax.all_gather(norm1_gain, "fsdp", axis=0, tiled=True),
        lax.all_gather(w_query, "fsdp", axis=0, tiled=True),
        lax.all_gather(w_key, "fsdp", axis=0, tiled=True),
        lax.all_gather(w_value, "fsdp", axis=0, tiled=True),
        lax.all_gather(w_out, "fsdp", axis=0, tiled=True),
    )
    gain_two, full_gate, full_up, full_down = (
        lax.all_gather(norm2_gain, "fsdp", axis=0, tiled=True),
        lax.all_gather(w_gate, "fsdp", axis=0, tiled=True),
        lax.all_gather(w_up, "fsdp", axis=0, tiled=True),
        lax.all_gather(w_down, "fsdp", axis=0, tiled=True),
    )
    grad_res = cotangent.astype(jnp.float32)
    grad_inner = jnp.einsum("td,fd->tf", cotangent, full_down, preferred_element_type=jnp.float32)
    grad_gate_low = (
        grad_inner * up_pre * sigmoid_gate * (1.0 + gate_pre * (1.0 - sigmoid_gate))
    ).astype(jnp.bfloat16)
    grad_up_low = (grad_inner * silu_gate).astype(jnp.bfloat16)
    grad_hidden_two = jnp.einsum(
        "tf,df->td", grad_gate_low, full_gate, preferred_element_type=jnp.float32
    )
    grad_hidden_two = grad_hidden_two + jnp.einsum(
        "tf,df->td", grad_up_low, full_up, preferred_element_type=jnp.float32
    )
    gain_two_local = jnp.sum(grad_hidden_two * normed_two, axis=0)
    grad_resid = grad_res + norm_back(
        grad_hidden_two, normed_two, scale_two, gain_two.astype(jnp.float32)
    )
    grad_attn_low = grad_resid.astype(jnp.bfloat16)
    grad_mix_low = jnp.einsum(
        "td,ed->te", grad_attn_low, full_out, preferred_element_type=jnp.float32
    ).astype(jnp.bfloat16)
    grad_mix_low = grad_mix_low * query_valid.astype(jnp.bfloat16)[:, None]
    grad_mix_grp = grad_mix_low.reshape(tok_rows, KVH, heads_per, HD).transpose(1, 0, 2, 3)

    def backward_entry(packed):
        return attend_backward(packed[0], packed[1], packed[2], allowed, packed[3], packed[4])

    grad_query_grp, grad_key_seq, grad_value_seq = lax.map(
        backward_entry, (query_grp, key_seq, value_seq, logsum, grad_mix_grp)
    )
    grad_queries = grad_query_grp.transpose(1, 0, 2, 3).reshape(tok_rows, H, HD)
    grad_query_low = (
        rotate_back(grad_queries, cos_table, sin_table)
        .reshape(tok_rows, H * HD)
        .astype(jnp.bfloat16)
    )
    kv_full = jnp.concatenate(
        [
            grad_key_seq.transpose(1, 0, 2).reshape(seq_len, kv_width),
            grad_value_seq.transpose(1, 0, 2).reshape(seq_len, kv_width),
        ],
        axis=1,
    )
    kv_grad = lax.psum_scatter(
        kv_full.astype(jnp.bfloat16), "fsdp", scatter_dimension=0, tiled=True
    ).astype(jnp.float32)
    grad_key_low = rotate_back(
        kv_grad[:, :kv_width].reshape(tok_rows, KVH, HD), cos_table, sin_table
    )
    grad_key_low = grad_key_low.reshape(tok_rows, kv_width).astype(jnp.bfloat16)
    grad_value_low = kv_grad[:, kv_width:].astype(jnp.bfloat16)
    grad_hidden_one = jnp.einsum(
        "te,de->td", grad_query_low, full_query, preferred_element_type=jnp.float32
    )
    grad_hidden_one = grad_hidden_one + jnp.einsum(
        "te,de->td", grad_key_low, full_key, preferred_element_type=jnp.float32
    )
    grad_hidden_one = grad_hidden_one + jnp.einsum(
        "te,de->td", grad_value_low, full_value, preferred_element_type=jnp.float32
    )
    gain_one_local = jnp.sum(grad_hidden_one * normed_one, axis=0)
    grad_inputs = (
        grad_resid + norm_back(grad_hidden_one, normed_one, scale_one, gain_one.astype(jnp.float32))
    ).astype(jnp.bfloat16)
    grad_qkv_cols = jnp.concatenate([grad_query_low, grad_key_low, grad_value_low], axis=1)
    grad_gate_up_cols = jnp.concatenate([grad_gate_low, grad_up_low], axis=1)
    gain_one_part, gain_two_part = (
        lax.psum_scatter(gain_one_local, "fsdp", scatter_dimension=0, tiled=True),
        lax.psum_scatter(gain_two_local, "fsdp", scatter_dimension=0, tiled=True),
    )
    part_qkv = lax.psum_scatter(
        jnp.einsum(
            "tc,tk->ck", hidden_one, grad_qkv_cols, preferred_element_type=jnp.float32
        ).astype(jnp.bfloat16),
        "fsdp",
        scatter_dimension=0,
        tiled=True,
    )
    part_out = lax.psum_scatter(
        jnp.einsum("tc,tk->ck", attn_low, grad_attn_low, preferred_element_type=jnp.float32).astype(
            jnp.bfloat16
        ),
        "fsdp",
        scatter_dimension=0,
        tiled=True,
    )
    part_gate_up = lax.psum_scatter(
        jnp.einsum(
            "tc,tk->ck", hidden_two, grad_gate_up_cols, preferred_element_type=jnp.float32
        ).astype(jnp.bfloat16),
        "fsdp",
        scatter_dimension=0,
        tiled=True,
    )
    part_down = lax.psum_scatter(
        jnp.einsum("tc,tk->ck", inner_low, cotangent, preferred_element_type=jnp.float32).astype(
            jnp.bfloat16
        ),
        "fsdp",
        scatter_dimension=0,
        tiled=True,
    )
    summed = (
        lax.psum(gain_one_part.astype(jnp.bfloat16), "rep").astype(jnp.float32),
        lax.psum(part_qkv, "rep").astype(jnp.float32),
        lax.psum(part_out, "rep").astype(jnp.float32),
        lax.psum(gain_two_part.astype(jnp.bfloat16), "rep").astype(jnp.float32),
        lax.psum(part_gate_up, "rep").astype(jnp.float32),
        lax.psum(part_down, "rep").astype(jnp.float32),
    )
    grad_norm_one, grad_qkv, grad_out_part, grad_norm_two, grad_gate_up, grad_down_part = summed
    grad_query_part = grad_qkv[:, :D]
    grad_key_part = grad_qkv[:, D : D + kv_width]
    grad_value_part = grad_qkv[:, D + kv_width :]
    grad_gate_part = grad_gate_up[:, :FF]
    grad_up_part = grad_gate_up[:, FF:]
    return (
        result,
        grad_inputs,
        grad_norm_one,
        grad_query_part,
        grad_key_part,
        grad_value_part,
        grad_out_part,
        grad_norm_two,
        grad_gate_part,
        grad_up_part,
        grad_down_part,
    )


def solution(mesh):
    placed = (
        P(("rep", "fsdp"), None),
        P(("rep", "fsdp"), None),
        P(),
        P("fsdp"),
        P("fsdp", None),
        P("fsdp", None),
        P("fsdp", None),
        P("fsdp", None),
        P("fsdp"),
        P("fsdp", None),
        P("fsdp", None),
        P("fsdp", None),
    )
    return jax.shard_map(
        local,
        mesh=mesh,
        in_specs=placed,
        out_specs=(
            P(("rep", "fsdp"), None),
            P(("rep", "fsdp"), None),
            P("fsdp"),
            P("fsdp", None),
            P("fsdp", None),
            P("fsdp", None),
            P("fsdp", None),
            P("fsdp"),
            P("fsdp", None),
            P("fsdp", None),
            P("fsdp", None),
        ),
        check_vma=False,
    )
```

profile of v0, /device:TPU:0, one launch (start us, length us, event | category | flops | bytes accessed | tf_op | source)
XLA Modules:
  0.0 1672.1 jit_solution(14276761914154948728)
XLA Ops:
  9.4 10.3 all-gather
  21.3 14.8 all-gather.13.cloned.1.call-done
  38.2 23.4 %all-gather.15.cloned.1.call-done = bf16[2048,256]{1,0:T(8,128)(2,1)} async-done(((bf16[256,256]{1,0:T(8,128)(2,1)}), bf16[2048,256]{1,0:T(8,128)(2,1)}) %all-gather.15.cloned.1.call-update) | async-done | bytes 1048592 | tf_op jit(solution)/shard_map/all_gather | solution.py:144
  67.7 8.8 all-gather.1
  76.5 11.1 all-gather.17.cloned.1.call-done
  89.3 54.5 %all-gather.11.cloned.1.call-done = bf16[2048,2048]{1,0:T(8,128)(2,1)} async-done(((bf16[256,2048]{1,0:T(8,128)(2,1)}), bf16[2048,2048]{1,0:T(8,128)(2,1)}) %all-gather.11.cloned.1.call-update) | async-done | bytes 8388624 | tf_op jit(solution)/shard_map/all_gather | solution.py:142
  143.7 6.9 fusion.108
  151.1 14.7 while.28
  168.4 31.5 %all-gather.19.cloned.1.call-done = bf16[2048,2048]{1,0:T(8,128)(2,1)} async-done(((bf16[256,2048]{1,0:T(8,128)(2,1)}), bf16[2048,2048]{1,0:T(8,128)(2,1)}) %all-gather.19.cloned.1.call-update) | async-done | bytes 8388624 | tf_op jit(solution)/shard_map/all_gather | solution.py:145
  204.8 113.3 %all-gather.21.cloned.1.call-done = bf16[2048,5632]{1,0:T(8,128)(2,1)} async-done(((bf16[256,5632]{1,0:T(8,128)(2,1)}), bf16[2048,5632]{1,0:T(8,128)(2,1)}) %all-gather.21.cloned.1.call-update) | async-done | bytes 23068688 | tf_op jit(solution)/shard_map/all_gather | solution.py:179
  318.1 12.3 fusion.117
  330.4 106.1 %all-gather.23.cloned.1.call-done = bf16[2048,5632]{1,0:T(8,128)(2,1)} async-done(((bf16[256,5632]{1,0:T(8,128)(2,1)}), bf16[2048,5632]{1,0:T(8,128)(2,1)}) %all-gather.23.cloned.1.call-update) | async-done | bytes 23068688 | tf_op jit(solution)/shard_map/all_gather | solution.py:180
  436.5 12.3 fusion.118
  448.8 106.1 %all-gather.25.cloned.1.call-done = bf16[5632,2048]{1,0:T(8,128)(2,1)} async-done(((bf16[704,2048]{1,0:T(8,128)(2,1)}), bf16[5632,2048]{1,0:T(8,128)(2,1)}) %all-gather.25.cloned.1.call-update) | async-done | bytes 23068688 | tf_op jit(solution)/shard_map/all_gather | solution.py:181
  554.9 15.0 multiply_convert_fusion.1
  569.8 12.3 fusion.119
  582.1 13.2 multiply_reduce_fusion.1
  597.1 7.1 fusion.71
  607.3 42.8 %while.29 = (s32[]{:T(128)}, f32[4,128,8,64]{1,3,2,0:T(8,128)}, bf16[4,1024,64]{1,2,0:T(8,128)(2,1)}, bf16[4,1024,64]{1,2,0:T(8,128)(2,1)}, bf16[4,128,8,64]{1,3...) while((s32[]{:T(128)}, f32[4,128,8,64]{1,3,2,0:T(8,128)}, ...), condition=%wide.region_11.12_spmd.clone, body=%wide.region_9.11_spmd.clone.sunk | while | flops 687864832 | bytes 44211620 | solution.py:232
  663.0 27.9 %reduce-scatter.16.cloned.1.call-done = bf16[128,512]{1,0:T(8,128)(2,1)} async-done(((bf16[1024,512]{1,0:T(8,128)(2,1)}), bf16[128,512]{1,0:T(8,128)(2,1)}) %reduce-scatter.16.cloned.1.call-update) | async-done | bytes 131088
  692.1 6.6 convolution_convert_fusion.2
  699.9 14.0 convolution_convert_fusion.1
  715.0 20.3 %convolution_convert_fusion = bf16[2048,11264]{1,0:T(8,128)(2,1)} fusion(bf16[128,2048]{1,0:T(8,128)(2,1)S(1)} %copy-done.9, bf16[128,5632]{1,0:T(8,128)(2,1)} %get-tuple-element.242, bf16[128,5632]{1,0:T(8,128)(2,1)} %get-tuple-element.243), kind=kOutput, calls=%fused_computation.73 | convolution fusion | flops 5934415872 | bytes 49545216 | tf_op jit(solution)/shard_map/tc,tk->ck/dot_general | solution.py:292
  735.6 29.9 %reduce-scatter.12.cloned.1.call-done = bf16[256,2048]{1,0:T(8,128)(2,1)} async-done(((bf16[2048,2048]{1,0:T(8,128)(2,1)}), bf16[256,2048]{1,0:T(8,128)(2,1)}) %reduce-scatter.12.cloned.1.call-update) | async-done | bytes 1048592 | tf_op jit(solution)/shard_map/reduce_scatter | solution.py:283
  765.5 85.5 %reduce-scatter.10.cloned.1.call-done = bf16[256,2560]{1,0:T(8,128)(2,1)} async-done(((bf16[2048,2560]{1,0:T(8,128)(2,1)}), bf16[256,2560]{1,0:T(8,128)(2,1)}) %reduce-scatter.10.cloned.1.call-update) | async-done | bytes 1310736 | tf_op jit(solution)/shard_map/reduce_scatter | solution.py:275
  851.0 149.8 %reduce-scatter.14.cloned.1.call-done = bf16[704,2048]{1,0:T(8,128)(2,1)} async-done(((bf16[5632,2048]{1,0:T(8,128)(2,1)}), bf16[704,2048]{1,0:T(8,128)(2,1)}) %reduce-scatter.14.cloned.1.call-update) | async-done | bytes 2883600 | tf_op jit(solution)/shard_map/reduce_scatter | solution.py:299
  1000.9 268.4 %reduce-scatter.18.cloned.1.call-done = bf16[256,11264]{1,0:T(8,128)(2,1)} async-done(((bf16[2048,11264]{1,0:T(8,128)(2,1)}), bf16[256,11264]{1,0:T(8,128)(2,1)}) %reduce-scatter.18.cloned.1.call-update) | async-done | bytes 5767184
  1271.2 6.4 fusion.120
  1277.7 12.0 fusion.70
  1290.8 25.4 %all-reduce.3 = (bf16[2048]{0:T(1024)(128)(2,1)S(1)}, bf16[2048]{0:T(1024)(128)(2,1)S(1)}) all-reduce(f32[2048]{0:T(1024)S(1)} %get-tuple-element.174, f32[2048]{0:T(1024)S(1)} %get-tuple-element.172), channel_id=3, replica_groups=mesh['rep'=4,'fsdp'=8] {'fsdp'}, use_global_device_ids=true, to_apply=%region_15.16.clone | all-reduce | flops 4096 | bytes 24576
  1316.4 12.4 all-reduce.4
  1331.1 318.6 %all-reduce.8.cloned.1.call-done = (bf16[256,2560]{1,0:T(8,128)(2,1)}, bf16[256,2048]{1,0:T(8,128)(2,1)}, bf16[256,11264]{1,0:T(8,128)(2,1)}, bf16[704,2048]{1,0:T(8,128)(2,1)}) async-done(((bf16[256,2560]{1,0:T(8,128)(2,1)}, bf16[256,2048]{1,0:T(8,128)(2,1)}, bf16[256,11264]{1,0:T(8,128)(2,1)}, bf16[704,2048]{1,0:T(8,128)(2,1)}), (bf16[256,2560]{1,0:T(8,128)(2,1)}, bf16[256,2048]{1,0:T(8,128)(2,1)}, ...) | async-done | bytes 11010064 | tf_op jit(solution)/shard_map/psum | solution.py:309
  (258 shorter events, 119.4 us)
Async XLA Ops:
  7.2 60.0 %copy-start = (s32[4,8]{1,0:T(4,128)S(1)}, s32[4,8]{1,0:T(4,128)}, u32[]{:S(2)}) copy-start(s32[4,8]{1,0:T(4,128)} %param.18) | copy-start | bytes 388
  7.2 54.4 %copy-start.3 = (bf16[128,2048]{1,0:T(8,128)(2,1)S(1)}, bf16[128,2048]{1,0:T(8,128)(2,1)}, u32[]{:S(2)}) copy-start(bf16[128,2048]{1,0:T(8,128)(2,1)} %param.16) | copy-start | bytes 1572868
  7.2 28.9 %all-gather.13.cloned.1.call-start = ((), (), s32[]{:S(2)}) async-start(), calls=%async_computation.6 | async-start | bytes 1179648 | tf_op jit(solution)/shard_map/all_gather | solution.py:143
  7.9 53.6 %all-gather.15.cloned.1.call-start = ((), (), s32[]{:S(2)}) async-start(), calls=%async_computation.7 | async-start | bytes 1179648 | tf_op jit(solution)/shard_map/all_gather | solution.py:144
  8.7 78.9 %all-gather.17.cloned.1.call-start = ((), (), s32[]{:S(2)}) async-start(), calls=%async_computation.8 | async-start | bytes 1179648 | tf_op jit(solution)/shard_map/all_gather | solution.py:164
  19.8 124.0 %copy-start.31 = (f32[8,1,256]{2,1,0:T(1,128)}, f32[8,1,256]{2,1,0:T(1,128)S(1)}, u32[]{:S(2)}) copy-start(f32[8,1,256]{2,1,0:T(1,128)S(1)} %convert_element_type.160) | copy-start | bytes 24580
  19.9 130.7 %copy-start.23 = (f32[128,64]{0,1:T(8,128)}, f32[128,64]{0,1:T(8,128)S(1)}, u32[]{:S(2)}) copy-start(f32[128,64]{0,1:T(8,128)S(1)} %get-tuple-element.260) | copy-start | bytes 98308
  20.0 130.7 %copy-start.25 = (f32[128,64]{0,1:T(8,128)}, f32[128,64]{0,1:T(8,128)S(1)}, u32[]{:S(2)}) copy-start(f32[128,64]{0,1:T(8,128)S(1)} %get-tuple-element.259) | copy-start | bytes 98308
  21.3 122.4 %copy-start.34 = (f32[128]{0:T(128)}, f32[128]{0:T(128)S(1)}, u32[]{:S(2)}) copy-start(f32[128]{0:T(128)S(1)} %add_rsqrt_fusion.1) | copy-start | bytes 1540
  63.8 79.9 %all-gather.11.cloned.1.call-start = ((), (), s32[]{:S(2)}) async-start(), calls=%async_computation.5 | async-start | bytes 9437184 | tf_op jit(solution)/shard_map/all_gather | solution.py:142
  64.4 135.5 %all-gather.19.cloned.1.call-start = ((), (), s32[]{:S(2)}) async-start(), calls=%async_computation.9 | async-start | bytes 9437184 | tf_op jit(solution)/shard_map/all_gather | solution.py:145
  65.0 253.1 %all-gather.21.cloned.1.call-start = ((), (), s32[]{:S(2)}) async-start(), calls=%async_computation.10 | async-start | bytes 25952256 | tf_op jit(solution)/shard_map/all_gather | solution.py:179
  65.6 370.9 %all-gather.23.cloned.1.call-start = ((), (), s32[]{:S(2)}) async-start(), calls=%async_computation.11 | async-start | bytes 25952256 | tf_op jit(solution)/shard_map/all_gather | solution.py:180
  66.4 488.5 %all-gather.25.cloned.1.call-start = ((), (), s32[]{:S(2)}) async-start(), calls=%async_computation.12 | async-start | bytes 25952256 | tf_op jit(solution)/shard_map/all_gather | solution.py:181
  67.1 623.8 %reduce-scatter.16.cloned.1.call-start = ((), (), s32[]{:S(2)}) async-start(), calls=%async_computation.16 | async-start | bytes 1179648
  168.4 36.2 %copy-start.6 = (bf16[128,2048]{0,1:T(8,128)(2,1)}, bf16[128,2048]{0,1:T(8,128)(2,1)S(1)}, u32[]{:S(2)}) copy-start(bf16[128,2048]{0,1:T(8,128)(2,1)S(1)} %fusion.88) | copy-start | bytes 1572868
  204.8 231.7 %copy-start.8 = (bf16[128,2048]{1,0:T(8,128)(2,1)}, bf16[128,2048]{1,0:T(8,128)(2,1)S(1)}, u32[]{:S(2)}) copy-start(bf16[128,2048]{1,0:T(8,128)(2,1)S(1)} %multiply_convert_fusion.4) | copy-start | bytes 1572868
  330.4 224.4 %copy-start.18 = (bf16[128,2048]{1,0:T(8,128)(2,1)S(1)}, bf16[128,2048]{1,0:T(8,128)(2,1)}, u32[]{:S(2)}) copy-start(bf16[128,2048]{1,0:T(8,128)(2,1)} %param.17) | copy-start | bytes 1572868
  569.8 12.3 copy-start.5
  654.7 110.8 %reduce-scatter.12.cloned.1.call-start = ((), (), s32[]{:S(2)}) async-start(), calls=%async_computation.14 | async-start | bytes 9437184 | tf_op jit(solution)/shard_map/reduce_scatter | solution.py:283
  660.5 190.6 %reduce-scatter.10.cloned.1.call-start = ((), (), s32[]{:S(2)}) async-start(), calls=%async_computation.13 | async-start | bytes 11796480 | tf_op jit(solution)/shard_map/reduce_scatter | solution.py:275
  662.6 29.5 %copy-start.32 = (f32[8,1,256]{2,1,0:T(1,128)S(1)}, f32[8,1,256]{2,1,0:T(1,128)}, u32[]{:S(2)}) copy-start(f32[8,1,256]{2,1,0:T(1,128)} %copy-done.31) | copy-start | bytes 24580
  662.6 29.5 %copy-start.35 = (f32[128]{0:T(128)S(1)}, f32[128]{0:T(128)}, u32[]{:S(2)}) copy-start(f32[128]{0:T(128)} %copy-done.34) | copy-start | bytes 1540
  663.0 35.8 %copy-start.12 = (bf16[128,2048]{0,1:T(8,128)(2,1)}, bf16[128,2048]{0,1:T(8,128)(2,1)S(1)}, u32[]{:S(2)}) copy-start(bf16[128,2048]{0,1:T(8,128)(2,1)S(1)} %fusion.87) | copy-start | bytes 1572868
  698.8 302.1 %reduce-scatter.14.cloned.1.call-start = ((), (), s32[]{:S(2)}) async-start(), calls=%async_computation.15 | async-start | bytes 25952256 | tf_op jit(solution)/shard_map/reduce_scatter | solution.py:299
  714.0 555.3 %reduce-scatter.18.cloned.1.call-start = ((), (), s32[]{:S(2)}) async-start(), calls=%async_computation.17 | async-start | bytes 51904512
  735.4 914.3 %all-reduce.8.cloned.1.call-start = ((), (), s32[]{:S(2)}) async-start(), calls=%async_computation.18 | async-start | bytes 22020096 | tf_op jit(solution)/shard_map/psum | solution.py:309
  1271.2 6.5 copy-start.11
  1277.6 12.1 copy-start.20
  1277.6 12.5 copy-start.22
  1277.7 12.5 copy-start.33
  1649.7 6.4 copy-start.2
  (35 other events, 74.7 us)
Sparse Core Ops, SparseCore 0:
  9.9 26.1 all-gather.12
  38.0 23.4 all-gather.14
  64.0 23.4 all-gather.16
  89.3 54.3 all-gather.10
  145.5 54.3 all-gather.18
  201.6 116.4 all-gather.20
  320.0 116.4 all-gather.22
  438.4 116.4 all-gather.24
  654.8 36.0 reduce-scatter.15
  694.2 71.2 reduce-scatter.11
  769.4 81.5 reduce-scatter.9
  854.9 145.8 reduce-scatter.13
  1004.9 264.2 reduce-scatter.17
  1272.0 377.6 all-reduce.7
where the time goes:
time: 1680 us; the launch traced here: 1670 us
  waiting for transfers between devices  1350 us (80%)
  matrix products  195 us (12%)
  blocking collectives  57 us (3%)
  other arithmetic  29.4 us (2%)
  local copies, waits for them, and re-layouts  28.5 us (2%)
    psum x1, waiting for transfers between devices, local(): lax.psum(part_qkv, 'rep').astype(jnp.float32)  319 us
    unnamed x16, waiting for transfers between devices  301 us
    reduce_scatter x1, waiting for transfers between devices, local(): lax.psum_scatter(jnp.einsum('tc,tk->ck', inner_low, cotangent, preferred_...  150 us
    all_gather x1, waiting for transfers between devices, local(): lax.all_gather(w_gate, 'fsdp', axis=0, tiled=True)  113 us
    all_gather x1, waiting for transfers between devices, local(): lax.all_gather(w_up, 'fsdp', axis=0, tiled=True)  106 us
    all_gather x1, waiting for transfers between devices, local(): lax.all_gather(w_down, 'fsdp', axis=0, tiled=True)  106 us
    reduce_scatter x1, waiting for transfers between devices, local(): lax.psum_scatter(jnp.einsum('tc,tk->ck', hidden_one, grad_qkv_cols, prefe...  85.5 us
    all_gather x1, waiting for transfers between devices, local(): lax.all_gather(w_query, 'fsdp', axis=0, tiled=True)  54.5 us
  transfers between devices with their start and end apart: 14, of which 14 were waited for; matrix products, arithmetic and copies ran while one was open for 8% of the time, Pallas kernels for 0%

commit v1 on v0

--- a/solution.py
+++ b/solution.py
@@ -306,7 +306,7 @@
     )
     summed = (
         lax.psum(gain_one_part.astype(jnp.bfloat16), "rep").astype(jnp.float32),
-        lax.psum(part_qkv, "rep").astype(jnp.float32),
+        jnp.sum(lax.all_gather(part_qkv, "rep"), axis=0).astype(jnp.float32),
         lax.psum(part_out, "rep").astype(jnp.float32),
         lax.psum(gain_two_part.astype(jnp.bfloat16), "rep").astype(jnp.float32),
         lax.psum(part_gate_up, "rep").astype(jnp.float32),

time: 1680 us -> 1740 us (1.036)
  waiting for transfers between devices: 1350 us -> 1400 us
    reduce_scatter x1, waiting for transfers between devices: 85.5 us -> 38 us  [local(): lax.psum_scatter(jnp.einsum('tc,tk->ck', hidden_one, grad_qkv_cols, prefe...]
    reduce_scatter x1, waiting for transfers between devices: 29.9 us -> 74.5 us  [local(): lax.psum_scatter(jnp.einsum('tc,tk->ck', attn_low, grad_attn_low, preferr...]
    all_gather x0 -> x1, waiting for transfers between devices: none -> 38 us  [local(): lax.all_gather(part_qkv, 'rep')]
    unnamed x16 -> x17, waiting for transfers between devices: 301 us -> 307 us
  transfers between devices with their start and end apart: 14 -> 15, of which waited for: 14 -> 15; matrix products, arithmetic and copies ran while one was open for 8% -> 8% of each run, Pallas kernels for 0% -> 0%
where the time goes in v1:
time: 1740 us; the launch traced here: 1730 us
  waiting for transfers between devices  1400 us (80%)
  matrix products  196 us (11%)
  blocking collectives  56.3 us (3%)
  other arithmetic  34.6 us (2%)
  local copies, waits for them, and re-layouts  29.2 us (2%)
    psum x1, waiting for transfers between devices, local(): lax.psum(part_out, 'rep').astype(jnp.float32)  329 us
    unnamed x17, waiting for transfers between devices  307 us
    reduce_scatter x1, waiting for transfers between devices, local(): lax.psum_scatter(jnp.einsum('tc,tk->ck', inner_low, cotangent, preferred_...  150 us
    all_gather x1, waiting for transfers between devices, local(): lax.all_gather(w_gate, 'fsdp', axis=0, tiled=True)  113 us
    all_gather x1, waiting for transfers between devices, local(): lax.all_gather(w_down, 'fsdp', axis=0, tiled=True)  106 us
    all_gather x1, waiting for transfers between devices, local(): lax.all_gather(w_up, 'fsdp', axis=0, tiled=True)  106 us
    reduce_scatter x1, waiting for transfers between devices, local(): lax.psum_scatter(jnp.einsum('tc,tk->ck', attn_low, grad_attn_low, preferr...  74.5 us
    all_gather x1, waiting for transfers between devices, local(): lax.all_gather(w_query, 'fsdp', axis=0, tiled=True)  54.5 us
  transfers between devices with their start and end apart: 15, of which 15 were waited for; matrix products, arithmetic and copies ran while one was open for 8% of the time, Pallas kernels for 0%

profile of v1, /device:TPU:0, one launch (start us, length us, event | category | flops | bytes accessed | tf_op | source)
XLA Modules:
  0.0 1730.5 jit_solution(1383590045544846180)
XLA Ops:
  9.4 10.3 all-gather.1
  21.3 14.8 all-gather.15.cloned.1.call-done
  38.2 23.4 %all-gather.17.cloned.1.call-done = bf16[2048,256]{1,0:T(8,128)(2,1)} async-done(((bf16[256,256]{1,0:T(8,128)(2,1)}), bf16[2048,256]{1,0:T(8,128)(2,1)}) %all-gather.17.cloned.1.call-update) | async-done | bytes 1048592 | tf_op jit(solution)/shard_map/all_gather | solution.py:144
  67.7 8.8 all-gather.2
  76.5 11.1 all-gather.19.cloned.1.call-done
  89.3 54.5 %all-gather.13.cloned.1.call-done = bf16[2048,2048]{1,0:T(8,128)(2,1)} async-done(((bf16[256,2048]{1,0:T(8,128)(2,1)}), bf16[2048,2048]{1,0:T(8,128)(2,1)}) %all-gather.13.cloned.1.call-update) | async-done | bytes 8388624 | tf_op jit(solution)/shard_map/all_gather | solution.py:142
  143.7 6.9 fusion.108
  151.1 14.7 while.28
  168.4 31.4 %all-gather.21.cloned.1.call-done = bf16[2048,2048]{1,0:T(8,128)(2,1)} async-done(((bf16[256,2048]{1,0:T(8,128)(2,1)}), bf16[2048,2048]{1,0:T(8,128)(2,1)}) %all-gather.21.cloned.1.call-update) | async-done | bytes 8388624 | tf_op jit(solution)/shard_map/all_gather | solution.py:145
  204.8 113.3 %all-gather.23.cloned.1.call-done = bf16[2048,5632]{1,0:T(8,128)(2,1)} async-done(((bf16[256,5632]{1,0:T(8,128)(2,1)}), bf16[2048,5632]{1,0:T(8,128)(2,1)}) %all-gather.23.cloned.1.call-update) | async-done | bytes 23068688 | tf_op jit(solution)/shard_map/all_gather | solution.py:179
  318.1 12.3 fusion.117
  330.4 106.1 %all-gather.25.cloned.1.call-done = bf16[2048,5632]{1,0:T(8,128)(2,1)} async-done(((bf16[256,5632]{1,0:T(8,128)(2,1)}), bf16[2048,5632]{1,0:T(8,128)(2,1)}) %all-gather.25.cloned.1.call-update) | async-done | bytes 23068688 | tf_op jit(solution)/shard_map/all_gather | solution.py:180
  436.5 12.3 fusion.118
  448.8 106.1 %all-gather.27.cloned.1.call-done = bf16[5632,2048]{1,0:T(8,128)(2,1)} async-done(((bf16[704,2048]{1,0:T(8,128)(2,1)}), bf16[5632,2048]{1,0:T(8,128)(2,1)}) %all-gather.27.cloned.1.call-update) | async-done | bytes 23068688 | tf_op jit(solution)/shard_map/all_gather | solution.py:181
  554.9 15.0 multiply_convert_fusion.1
  569.8 12.2 fusion.119
  582.1 13.2 multiply_reduce_fusion.1
  597.1 7.1 fusion.71
  607.3 42.8 %while.29 = (s32[]{:T(128)}, f32[4,128,8,64]{1,3,2,0:T(8,128)}, bf16[4,1024,64]{1,2,0:T(8,128)(2,1)}, bf16[4,1024,64]{1,2,0:T(8,128)(2,1)}, bf16[4,128,8,64]{1,3...) while((s32[]{:T(128)}, f32[4,128,8,64]{1,3,2,0:T(8,128)}, ...), condition=%wide.region_11.12_spmd.clone, body=%wide.region_9.11_spmd.clone.sunk | while | flops 687864832 | bytes 44211620 | solution.py:232
  656.6 34.3 %reduce-scatter.16.cloned.1.call-done = bf16[128,512]{1,0:T(8,128)(2,1)} async-done(((bf16[1024,512]{1,0:T(8,128)(2,1)}), bf16[128,512]{1,0:T(8,128)(2,1)}) %reduce-scatter.16.cloned.1.call-update) | async-done | bytes 131088
  707.0 14.1 convolution_convert_fusion.1
  722.1 20.4 %convolution_convert_fusion = bf16[2048,11264]{1,0:T(8,128)(2,1)} fusion(bf16[128,2048]{1,0:T(8,128)(2,1)S(1)} %copy-done.8, bf16[128,5632]{1,0:T(8,128)(2,1)} %get-tuple-element.241, bf16[128,5632]{1,0:T(8,128)(2,1)} %get-tuple-element.242), kind=kOutput, calls=%fused_computation.73 | convolution fusion | flops 5934415872 | bytes 49545216 | tf_op jit(solution)/shard_map/tc,tk->ck/dot_general | solution.py:292
  742.6 38.0 %reduce-scatter.10.cloned.1.call-done = bf16[256,2560]{1,0:T(8,128)(2,1)} async-done(((bf16[2048,2560]{1,0:T(8,128)(2,1)}), bf16[256,2560]{1,0:T(8,128)(2,1)}) %reduce-scatter.10.cloned.1.call-update) | async-done | bytes 1310736 | tf_op jit(solution)/shard_map/reduce_scatter | solution.py:275
  780.9 74.5 %reduce-scatter.12.cloned.1.call-done = bf16[256,2048]{1,0:T(8,128)(2,1)} async-done(((bf16[2048,2048]{1,0:T(8,128)(2,1)}), bf16[256,2048]{1,0:T(8,128)(2,1)}) %reduce-scatter.12.cloned.1.call-update) | async-done | bytes 1048592 | tf_op jit(solution)/shard_map/reduce_scatter | solution.py:283
  855.3 149.8 %reduce-scatter.14.cloned.1.call-done = bf16[704,2048]{1,0:T(8,128)(2,1)} async-done(((bf16[5632,2048]{1,0:T(8,128)(2,1)}), bf16[704,2048]{1,0:T(8,128)(2,1)}) %reduce-scatter.14.cloned.1.call-update) | async-done | bytes 2883600 | tf_op jit(solution)/shard_map/reduce_scatter | solution.py:299
  1005.2 268.4 %reduce-scatter.18.cloned.1.call-done = bf16[256,11264]{1,0:T(8,128)(2,1)} async-done(((bf16[2048,11264]{1,0:T(8,128)(2,1)}), bf16[256,11264]{1,0:T(8,128)(2,1)}) %reduce-scatter.18.cloned.1.call-update) | async-done | bytes 5767184
  1282.0 12.6 fusion.70
  1295.7 25.1 %all-reduce.3 = (bf16[2048]{0:T(1024)(128)(2,1)S(1)}, bf16[2048]{0:T(1024)(128)(2,1)S(1)}) all-reduce(f32[2048]{0:T(1024)S(1)} %get-tuple-element.174, f32[2048]{0:T(1024)S(1)} %get-tuple-element.172), channel_id=4, replica_groups=mesh['rep'=4,'fsdp'=8] {'fsdp'}, use_global_device_ids=true, to_apply=%region_15.16.clone | all-reduce | flops 4096 | bytes 24576
  1321.0 12.1 all-reduce.4
  1335.3 38.0 %all-gather.29.cloned.1.call-done = bf16[1024,2560]{1,0:T(8,128)(2,1)} async-done(((bf16[256,2560]{1,0:T(8,128)(2,1)}), bf16[1024,2560]{1,0:T(8,128)(2,1)}) %all-gather.29.cloned.1.call-update) | async-done | bytes 5242896 | tf_op jit(solution)/shard_map/all_gather | solution.py:309
  1379.7 329.2 %all-reduce.8.cloned.1.call-done = (bf16[256,2048]{1,0:T(8,128)(2,1)}, bf16[256,11264]{1,0:T(8,128)(2,1)}, bf16[704,2048]{1,0:T(8,128)(2,1)}) async-done(((bf16[256,2048]{1,0:T(8,128)(2,1)}, bf16[256,11264]{1,0:T(8,128)(2,1)}, bf16[704,2048]{1,0:T(8,128)(2,1)}), (bf16[256,2048]{1,0:T(8,128)(2,1)}, bf16[256,11264]{1,0:T(8,128)(2,1)}, bf16[704,2048]{1,0:T(8,128)(2,1)})) %all-reduce.8.cloned.1.call-update) | async-done | bytes 9699344 | tf_op jit(solution)/shard_map/psum | solution.py:310
  1711.6 8.8 fusion.111
  (258 shorter events, 130.1 us)
Async XLA Ops:
  7.2 60.0 %copy-start = (s32[4,8]{1,0:T(4,128)S(1)}, s32[4,8]{1,0:T(4,128)}, u32[]{:S(2)}) copy-start(s32[4,8]{1,0:T(4,128)} %param.18) | copy-start | bytes 388
  7.2 54.4 %copy-start.2 = (bf16[128,2048]{1,0:T(8,128)(2,1)S(1)}, bf16[128,2048]{1,0:T(8,128)(2,1)}, u32[]{:S(2)}) copy-start(bf16[128,2048]{1,0:T(8,128)(2,1)} %param.16) | copy-start | bytes 1572868
  7.2 28.9 %all-gather.15.cloned.1.call-start = ((), (), s32[]{:S(2)}) async-start(), calls=%async_computation.6 | async-start | bytes 1179648 | tf_op jit(solution)/shard_map/all_gather | solution.py:143
  7.9 53.6 %all-gather.17.cloned.1.call-start = ((), (), s32[]{:S(2)}) async-start(), calls=%async_computation.7 | async-start | bytes 1179648 | tf_op jit(solution)/shard_map/all_gather | solution.py:144
  8.7 78.9 %all-gather.19.cloned.1.call-start = ((), (), s32[]{:S(2)}) async-start(), calls=%async_computation.8 | async-start | bytes 1179648 | tf_op jit(solution)/shard_map/all_gather | solution.py:164
  19.8 124.0 %copy-start.29 = (f32[8,1,256]{2,1,0:T(1,128)}, f32[8,1,256]{2,1,0:T(1,128)S(1)}, u32[]{:S(2)}) copy-start(f32[8,1,256]{2,1,0:T(1,128)S(1)} %convert_element_type.162) | copy-start | bytes 24580
  19.9 130.8 %copy-start.21 = (f32[128,64]{0,1:T(8,128)}, f32[128,64]{0,1:T(8,128)S(1)}, u32[]{:S(2)}) copy-start(f32[128,64]{0,1:T(8,128)S(1)} %get-tuple-element.259) | copy-start | bytes 98308
  20.0 130.8 %copy-start.23 = (f32[128,64]{0,1:T(8,128)}, f32[128,64]{0,1:T(8,128)S(1)}, u32[]{:S(2)}) copy-start(f32[128,64]{0,1:T(8,128)S(1)} %get-tuple-element.258) | copy-start | bytes 98308
  21.3 122.4 %copy-start.32 = (f32[128]{0:T(128)}, f32[128]{0:T(128)S(1)}, u32[]{:S(2)}) copy-start(f32[128]{0:T(128)S(1)} %add_rsqrt_fusion.1) | copy-start | bytes 1540
  63.8 79.9 %all-gather.13.cloned.1.call-start = ((), (), s32[]{:S(2)}) async-start(), calls=%async_computation.5 | async-start | bytes 9437184 | tf_op jit(solution)/shard_map/all_gather | solution.py:142
  64.4 135.5 %all-gather.21.cloned.1.call-start = ((), (), s32[]{:S(2)}) async-start(), calls=%async_computation.9 | async-start | bytes 9437184 | tf_op jit(solution)/shard_map/all_gather | solution.py:145
  65.0 253.1 %all-gather.23.cloned.1.call-start = ((), (), s32[]{:S(2)}) async-start(), calls=%async_computation.10 | async-start | bytes 25952256 | tf_op jit(solution)/shard_map/all_gather | solution.py:179
  65.6 370.9 %all-gather.25.cloned.1.call-start = ((), (), s32[]{:S(2)}) async-start(), calls=%async_computation.11 | async-start | bytes 25952256 | tf_op jit(solution)/shard_map/all_gather | solution.py:180
  66.4 488.5 %all-gather.27.cloned.1.call-start = ((), (), s32[]{:S(2)}) async-start(), calls=%async_computation.12 | async-start | bytes 25952256 | tf_op jit(solution)/shard_map/all_gather | solution.py:181
  67.1 623.8 %reduce-scatter.16.cloned.1.call-start = ((), (), s32[]{:S(2)}) async-start(), calls=%async_computation.17 | async-start | bytes 1179648
  168.4 36.2 %copy-start.5 = (bf16[128,2048]{0,1:T(8,128)(2,1)}, bf16[128,2048]{0,1:T(8,128)(2,1)S(1)}, u32[]{:S(2)}) copy-start(bf16[128,2048]{0,1:T(8,128)(2,1)S(1)} %fusion.88) | copy-start | bytes 1572868
  204.8 231.7 %copy-start.7 = (bf16[128,2048]{1,0:T(8,128)(2,1)}, bf16[128,2048]{1,0:T(8,128)(2,1)S(1)}, u32[]{:S(2)}) copy-start(bf16[128,2048]{1,0:T(8,128)(2,1)S(1)} %multiply_convert_fusion.4) | copy-start | bytes 1572868
  330.4 224.4 %copy-start.17 = (bf16[128,2048]{1,0:T(8,128)(2,1)S(1)}, bf16[128,2048]{1,0:T(8,128)(2,1)}, u32[]{:S(2)}) copy-start(bf16[128,2048]{1,0:T(8,128)(2,1)} %param.17) | copy-start | bytes 1572868
  569.8 12.3 copy-start.4
  654.7 125.9 %reduce-scatter.10.cloned.1.call-start = ((), (), s32[]{:S(2)}) async-start(), calls=%async_computation.13 | async-start | bytes 11796480 | tf_op jit(solution)/shard_map/reduce_scatter | solution.py:275
  656.2 35.9 %copy-start.30 = (f32[8,1,256]{2,1,0:T(1,128)S(1)}, f32[8,1,256]{2,1,0:T(1,128)}, u32[]{:S(2)}) copy-start(f32[8,1,256]{2,1,0:T(1,128)} %copy-done.29) | copy-start | bytes 24580
  656.3 35.9 %copy-start.33 = (f32[128]{0:T(128)S(1)}, f32[128]{0:T(128)}, u32[]{:S(2)}) copy-start(f32[128]{0:T(128)} %copy-done.32) | copy-start | bytes 1540
  656.6 42.3 %copy-start.11 = (bf16[128,2048]{0,1:T(8,128)(2,1)}, bf16[128,2048]{0,1:T(8,128)(2,1)S(1)}, u32[]{:S(2)}) copy-start(bf16[128,2048]{0,1:T(8,128)(2,1)S(1)} %fusion.87) | copy-start | bytes 1572868
  698.9 156.5 %reduce-scatter.12.cloned.1.call-start = ((), (), s32[]{:S(2)}) async-start(), calls=%async_computation.14 | async-start | bytes 9437184 | tf_op jit(solution)/shard_map/reduce_scatter | solution.py:283
  705.9 299.3 %reduce-scatter.14.cloned.1.call-start = ((), (), s32[]{:S(2)}) async-start(), calls=%async_computation.15 | async-start | bytes 25952256 | tf_op jit(solution)/shard_map/reduce_scatter | solution.py:299
  721.1 552.5 %reduce-scatter.18.cloned.1.call-start = ((), (), s32[]{:S(2)}) async-start(), calls=%async_computation.18 | async-start | bytes 51904512
  742.5 630.8 %all-gather.29.cloned.1.call-start = ((), (), s32[]{:S(2)}) async-start(), calls=%async_computation.16 | async-start | bytes 6553600 | tf_op jit(solution)/shard_map/all_gather | solution.py:309
  780.6 928.2 %all-reduce.8.cloned.1.call-start = ((), (), s32[]{:S(2)}) async-start(), calls=%async_computation.19 | async-start | bytes 19398656 | tf_op jit(solution)/shard_map/psum | solution.py:310
  1281.9 12.6 copy-start.19
  1282.0 13.1 copy-start.20
  1282.0 13.1 copy-start.31
  1711.6 8.8 copy-start.14
  (34 other events, 69.4 us)
Sparse Core Ops, SparseCore 0:
  9.9 26.1 all-gather.14
  38.0 23.4 all-gather.16
  64.0 23.4 all-gather.18
  89.3 54.3 all-gather.12
  145.5 54.3 all-gather.20
  201.6 116.4 all-gather.22
  320.0 116.4 all-gather.24
  438.4 116.4 all-gather.26
  654.8 36.0 reduce-scatter.15
  699.0 81.5 reduce-scatter.9
  784.1 71.2 reduce-scatter.11
  859.3 145.8 reduce-scatter.13
  1009.2 264.2 reduce-scatter.17
  1275.0 98.2 all-gather.28
  1376.0 332.8 all-reduce.7
